TPU v7x, 32 devices: a whole 2x2x4 slice. The times are simulated.
32 devices in a mesh: row: 4 (over z), col: 8 (over y, x, core).
Axes of the slice: x: 2, y: 2, z: 4, core: 2. Of those that a mesh axis runs over, the one named last changes fastest.
Arguments:
- cotangent: float32 [4096, 8192], P('row', 'col'), may hold values from -6 to 6
- whitened: float32 [4096, 8192], P('row', 'col'), may hold values from -0.0625 to 0.0625
- panel_rows: float32 [4, 256, 4096], P(None, None, 'row'), may hold values from -0.375 to 0.375
- diag_inverse: float32 [4, 256, 256], replicated, as said below
Outputs:
- adjoint_rhs: float32 [4096, 8192], P('row', 'col')
- factor_grad: float32 [4, 256, 4096], P(None, 'col', 'row')
Inputs may be any that keep to these rules, and one draw needn't show every extreme that they name: `diag_inverse`: each block is lower triangular with diagonal entries between 0.5 and 1.5.
All inputs are finite; a program needn't handle non-finite values.
Results may differ from a plain program's by a relative error of at most 0.00017.
Values sent between devices are 32-bit elements; how exact they have to be, the bound alone decides.
A program may use at most 128 MiB of HBM per device.

v0:
```python
import jax
import jax.numpy as jnp
from jax import lax
from jax.sharding import PartitionSpec as P


def broadcast(array, axis, root):
    mine = lax.axis_index(axis) == root
    return lax.psum(jnp.where(mine, array, jnp.zeros_like(array)), axis)


def grad_mask(count, natural, within, target):
    inner = jnp.arange(count, dtype=jnp.int32)
    return (natural[None, :] < target) | (natural[None, :] == target) & (
        inner[:, None] >= within[None, :]
    )


def body(cotangent, whitened, panel_rows, diag_inverse):
    hi = lax.Precision.HIGHEST
    n_row = lax.axis_size("row")
    rows_dev = cotangent.shape[0]
    width = diag_inverse.shape[1]
    panel_count = panel_rows.shape[0]
    blocks = rows_dev // width * n_row
    device = lax.axis_index("row")
    local = jnp.arange(rows_dev, dtype=jnp.int32)
    natural = local // width * n_row + device
    within = local % width
    residual = cotangent
    terms = []
    for p in range(panel_count):
        target = blocks - 1 - p
        root = n_row - 1 - p
        own = residual[rows_dev - width :]
        solved = jnp.dot(diag_inverse[p].T, own, precision=hi, preferred_element_type=jnp.float32)
        solved = broadcast(solved, "row", root)
        masked = jnp.where((natural < target)[None, :], panel_rows[p], 0.0)
        update = lax.dot_general(
            masked,
            solved,
            (((0,), (0,)), ((), ())),
            precision=hi,
            preferred_element_type=jnp.float32,
        )
        residual = residual - update
        tail = jnp.where(device == root, solved, residual[rows_dev - width :])
        residual = jnp.concatenate([residual[: rows_dev - width], tail], 0)
        partial_term = lax.dot_general(
            solved,
            whitened,
            (((1,), (1,)), ((), ())),
            precision=hi,
            preferred_element_type=jnp.float32,
        )
        terms.append(jnp.where(grad_mask(width, natural, within, target), -partial_term, 0.0))
    factor_grad = lax.psum_scatter(jnp.stack(terms), "col", scatter_dimension=1, tiled=True)
    return (residual, factor_grad)


def solution(mesh):
    return jax.shard_map(
        body,
        mesh=mesh,
        in_specs=(P("row", "col"), P("row", "col"), P(None, None, "row"), P()),
        out_specs=(P("row", "col"), P(None, "col", "row")),
        check_vma=False,
    )
```

profile of v0, /device:TPU:0, one launch (start us, length us, event | category | flops | bytes accessed | tf_op | source)
XLA Modules:
  0.0 321.2 jit_solution(1200197251109899264)
XLA Ops:
  7.2 0.0 all-reduce.5.cloned.1.call-start
  7.2 3.3 %convolution_select_fusion.3 = f32[256,1024]{1,0:T(8,128)} fusion(f32[1024,1024]{1,0:T(8,128)} %param.4, pred[]{:T(512)S(6)} %eq.50, f32[4,256,256]{2,1,0:T(8,128)} %param.7), kind=kOutput, calls=%fused_computation.12 | convolution fusion | flops 805568512 | bytes 2359297 | tf_op jit(solution)/shard_map/dot_general | solution.py:36
  10.5 0.0 all-reduce.5.cloned.1.call-update
  10.6 0.0 all-reduce.7.cloned.1.call-start
  10.6 54.9 %all-reduce.5.cloned.1.call-done = f32[256,1024]{1,0:T(8,128)} async-done(((f32[256,1024]{1,0:T(8,128)}), f32[256,1024]{1,0:T(8,128)}) %all-reduce.5.cloned.1.call-update) | async-done | bytes 1048592 | tf_op jit(solution)/shard_map/psum | solution.py:9
  65.6 0.0 copy-start.4
  65.6 6.7 %convolution_subtract_fusion = f32[1024,1024]{1,0:T(8,128)S(1)} fusion(f32[1024,1024]{1,0:T(8,128)} %param.4, f32[256,1024]{1,0:T(8,128)} %all-reduce.5.cloned.1.call-done, f32[4,256,1024]{2,1,0:T(8,128)} %param.6, pred[1024]{0:T(1024)(128)(4,1)S(1)} %fusion.56), kind=kOutput, calls=%fused_computation.5 | convolution fusion | flops 3222536192 | bytes 10486784 | tf_op jit(solution)/shard_map/dot_general | solution.py:39
  72.3 0.0 copy-start.3
  72.3 2.0 copy-done.3
  74.3 0.0 copy-done.4
  74.3 0.1 slice_select_fusion.3
  74.4 0.0 copy-start.12
  74.4 1.0 copy-done.12
  75.4 3.0 fusion.2
  78.5 0.0 slice-start.2
  78.5 0.0 all-reduce.7.cloned.1.call-update
  78.5 0.0 all-reduce.9.cloned.1.call-start
  78.6 51.2 %all-reduce.7.cloned.1.call-done = f32[256,1024]{1,0:T(8,128)} async-done(((f32[256,1024]{1,0:T(8,128)}), f32[256,1024]{1,0:T(8,128)}) %all-reduce.7.cloned.1.call-update) | async-done | bytes 1048592 | tf_op jit(solution)/shard_map/psum | solution.py:9
  129.8 0.0 slice-done.2
  129.8 0.0 copy-start.6
  129.8 5.8 %maximum_subtract_fusion = f32[1024,1024]{1,0:T(8,128)S(1)} fusion(f32[256,1024]{1,0:T(8,128)} %copy-done.12, f32[768,1024]{1,0:T(8,128)S(1)} %slice-done.2, f32[256,1024]{1,0:T(8,128)} %all-reduce.7.cloned.1.call-done, f32[4,256,1024]{2,1,0:T(8,128)} %param.6, pred[1024]{0:T(1024)(128)(4,1)S(1)} %fusion.55), kind=kOutput, calls=%fused_computation | convolution fusion | flops 3223584768 | bytes 10486784 | tf_op jit(solution)/shard_map/dot_general | solution.py:39
  135.6 0.0 copy-start.2
  135.6 2.0 copy-done.2
  137.6 0.0 copy-done.6
  137.6 0.1 slice_select_fusion.2
  137.7 0.0 copy-start.11
  137.8 1.0 copy-done.11
  138.7 3.1 fusion.1
  141.8 0.0 all-reduce.9.cloned.1.call-update
  141.8 0.2 all-reduce.11.cloned.1.call-start
  142.1 51.0 %all-reduce.9.cloned.1.call-done = f32[256,1024]{1,0:T(8,128)} async-done(((f32[256,1024]{1,0:T(8,128)}), f32[256,1024]{1,0:T(8,128)}) %all-reduce.9.cloned.1.call-update) | async-done | bytes 1048592 | tf_op jit(solution)/shard_map/psum | solution.py:9
  193.1 0.0 slice-done.1
  193.1 5.8 %maximum_subtract_fusion.1 = f32[1024,1024]{1,0:T(8,128)S(1)} fusion(f32[256,1024]{1,0:T(8,128)} %copy-done.11, f32[768,1024]{1,0:T(8,128)S(1)} %slice-done.1, f32[256,1024]{1,0:T(8,128)} %all-reduce.9.cloned.1.call-done, f32[4,256,1024]{2,1,0:T(8,128)} %param.6, pred[1024]{0:T(1024)(128)(4,1)S(1)} %fusion.54), kind=kOutput, calls=%fused_computation.1 | convolution fusion | flops 3223584768 | bytes 10486784 | tf_op jit(solution)/shard_map/dot_general | solution.py:39
  198.9 0.0 copy-start.1
  198.9 2.0 copy-done.1
  200.9 0.0 copy-done.9
  200.9 0.1 slice_select_fusion.1
  201.1 3.1 fusion
  204.2 0.0 all-reduce.11.cloned.1.call-update
  204.2 0.0 reduce-scatter.2.cloned.1.call-start
  204.3 0.0 copy-start
  204.3 0.0 copy-done.5
  204.3 7.1 %fusion.10 = f32[1,256,1024]{2,1,0:T(8,128)} fusion(f32[256,1024]{1,0:T(8,128)S(1)} %copy-done.5, f32[1024,1024]{1,0:T(8,128)} %param.5, s32[1024]{0:T(1024)S(1)} %fusion.40, pred[1024]{0:T(1024)(128)(4,1)S(1)} %get-tuple-element.5, pred[1024]{0:T(1024)(128)(4,1)S(1)} %fusion.56), kind=kOutput, calls=%fused_computation.24 | convolution fusion | flops 3222536192 | bytes 6297600 | tf_op jit(solution)/shard_map/dot_general | solution.py:49
  211.4 0.0 copy-done.7
  211.4 0.0 copy-done
  211.4 4.8 %fusion.8 = f32[1,256,1024]{2,1,0:T(8,128)} fusion(f32[256,1024]{1,0:T(8,128)S(1)} %copy-done.7, f32[1024,1024]{1,0:T(8,128)S(1)} %copy-done, s32[1024]{0:T(1024)S(1)} %fusion.40, pred[1024]{0:T(1024)(128)(4,1)S(1)} %get-tuple-element.4, pred[1024]{0:T(1024)(128)(4,1)S(1)} %fusion.55), kind=kOutput, calls=%fused_computation.21 | convolution fusion | flops 3222536192 | bytes 6297600 | tf_op jit(solution)/shard_map/dot_general | solution.py:49
  216.1 0.0 copy-done.10
  216.1 4.8 %fusion.6 = f32[1,256,1024]{2,1,0:T(8,128)} fusion(f32[256,1024]{1,0:T(8,128)S(1)} %copy-done.10, f32[1024,1024]{1,0:T(8,128)S(1)} %copy-done, s32[1024]{0:T(1024)S(1)} %fusion.40, pred[1024]{0:T(1024)(128)(4,1)S(1)} %get-tuple-element.3, pred[1024]{0:T(1024)(128)(4,1)S(1)} %fusion.54), kind=kOutput, calls=%fused_computation.18 | convolution fusion | flops 3222536192 | bytes 6297600 | tf_op jit(solution)/shard_map/dot_general | solution.py:49
  220.9 34.6 %all-reduce.11.cloned.1.call-done = f32[256,1024]{1,0:T(8,128)} async-done(((f32[256,1024]{1,0:T(8,128)}), f32[256,1024]{1,0:T(8,128)}) %all-reduce.11.cloned.1.call-update) | async-done | bytes 1048592 | tf_op jit(solution)/shard_map/psum | solution.py:9
  255.5 6.2 %fusion.4 = f32[1,256,1024]{2,1,0:T(8,128)S(1)} fusion(f32[256,1024]{1,0:T(8,128)} %all-reduce.11.cloned.1.call-done, f32[1024,1024]{1,0:T(8,128)} %param.5, s32[1024]{0:T(1024)S(1)} %fusion.40, pred[1024]{0:T(1024)(128)(4,1)S(1)} %get-tuple-element.2, pred[1024]{0:T(1024)(128)(4,1)S(1)} %fusion.53), kind=kOutput, calls=%fused_computation.15 | convolution fusion | flops 3222536192 | bytes 6297600 | tf_op jit(solution)/shard_map/dot_general | solution.py:49
  261.7 0.0 copy-done.13
  261.8 0.0 copy-done.14
  261.8 0.0 copy-done.15
  261.8 2.3 pad_maximum_fusion.1
  264.0 0.0 reduce-scatter.2.cloned.1.call-update
  264.1 0.0 slice-start
  264.1 0.0 copy-start.8
  264.1 1.9 slice-done
  266.0 0.3 copy-done.8
  266.2 5.0 %maximum_subtract_fusion.2 = f32[1024,1024]{1,0:T(8,128)S(1)} fusion(f32[256,1024]{1,0:T(8,128)S(1)} %slice_select_fusion.1, f32[768,1024]{1,0:T(8,128)S(1)} %slice-done, f32[256,1024]{1,0:T(8,128)S(1)} %copy-done.8, f32[4,256,1024]{2,1,0:T(8,128)} %param.6, pred[1024]{0:T(1024)(128)(4,1)S(1)} %fusion.53), kind=kOutput, calls=%fused_computation.2 | convolution fusion | flops 3223584768 | bytes 10486784 | tf_op jit(solution)/shard_map/dot_general | solution.py:39
  271.3 0.4 slice.74
  271.7 0.2 slice_select_fusion
  271.8 2.3 pad_maximum_fusion
  274.2 40.5 %reduce-scatter.2.cloned.1.call-done = f32[4,32,1024]{2,1,0:T(8,128)} async-done(((f32[4,256,1024]{2,1,0:T(8,128)}), f32[4,32,1024]{2,1,0:T(8,128)}) %reduce-scatter.2.cloned.1.call-update) | async-done | bytes 524304 | tf_op jit(solution)/shard_map/reduce_scatter | solution.py:57
  (15 shorter events, 0.1 us)
Async XLA Ops:
  7.2 58.4 %all-reduce.5.cloned.1.call-start = ((), (), s32[]{:S(2)}) async-start(), calls=%async_computation.1 | async-start | bytes 2097152 | tf_op jit(solution)/shard_map/psum | solution.py:9
  10.6 119.2 %all-reduce.7.cloned.1.call-start = ((), (), s32[]{:S(2)}) async-start(), calls=%async_computation.2 | async-start | bytes 2097152 | tf_op jit(solution)/shard_map/psum | solution.py:9
  65.6 8.7 %copy-start.4 = (f32[256,1024]{1,0:T(8,128)S(1)}, f32[256,1024]{1,0:T(8,128)}, u32[]{:S(2)}) copy-start(f32[256,1024]{1,0:T(8,128)} %all-reduce.5.cloned.1.call-done) | copy-start | bytes 3145732
  72.3 2.0 copy-start.3
  74.4 1.0 copy-start.12
  78.5 51.3 %slice-start.2 = ((f32[1024,1024]{1,0:T(8,128)}), f32[768,1024]{1,0:T(8,128)S(1)}, s32[]{:S(2)}) async-start(f32[1024,1024]{1,0:T(8,128)} %copy-done.3), calls=%async_computation.8 | async-start | bytes 6291456 | tf_op jit(solution)/shard_map/slice | solution.py:48
  78.5 114.6 %all-reduce.9.cloned.1.call-start = ((), (), s32[]{:S(2)}) async-start(), calls=%async_computation.3 | async-start | bytes 2097152 | tf_op jit(solution)/shard_map/psum | solution.py:9
  129.8 7.8 %copy-start.6 = (f32[256,1024]{1,0:T(8,128)S(1)}, f32[256,1024]{1,0:T(8,128)}, u32[]{:S(2)}) copy-start(f32[256,1024]{1,0:T(8,128)} %all-reduce.7.cloned.1.call-done) | copy-start | bytes 3145732
  135.6 2.0 copy-start.2
  137.7 1.0 copy-start.11
  141.8 51.3 %slice-start.1 = ((f32[1024,1024]{1,0:T(8,128)}), f32[768,1024]{1,0:T(8,128)S(1)}, s32[]{:S(2)}) async-start(f32[1024,1024]{1,0:T(8,128)} %copy-done.2), calls=%async_computation.7 | async-start | bytes 6291456 | tf_op jit(solution)/shard_map/slice | solution.py:48
  141.8 113.7 %all-reduce.11.cloned.1.call-start = ((), (), s32[]{:S(2)}) async-start(), calls=%async_computation.4 | async-start | bytes 2097152 | tf_op jit(solution)/shard_map/psum | solution.py:9
  193.1 7.8 %copy-start.9 = (f32[256,1024]{1,0:T(8,128)S(1)}, f32[256,1024]{1,0:T(8,128)}, u32[]{:S(2)}) copy-start(f32[256,1024]{1,0:T(8,128)} %all-reduce.9.cloned.1.call-done) | copy-start | bytes 3145732
  198.9 2.0 copy-start.1
  200.9 3.4 %copy-start.5 = (f32[256,1024]{1,0:T(8,128)S(1)}, f32[256,1024]{1,0:T(8,128)}, u32[]{:S(2)}) copy-start(f32[256,1024]{1,0:T(8,128)} %all-reduce.5.cloned.1.call-done) | copy-start | bytes 3145732
  204.2 7.2 %copy-start.7 = (f32[256,1024]{1,0:T(8,128)S(1)}, f32[256,1024]{1,0:T(8,128)}, u32[]{:S(2)}) copy-start(f32[256,1024]{1,0:T(8,128)} %all-reduce.7.cloned.1.call-done) | copy-start | bytes 3145732
  204.2 110.4 %reduce-scatter.2.cloned.1.call-start = ((), (), s32[]{:S(2)}) async-start(), calls=%async_computation.5 | async-start | bytes 4718592 | tf_op jit(solution)/shard_map/reduce_scatter | solution.py:57
  204.3 7.1 %copy-start = (f32[1024,1024]{1,0:T(8,128)S(1)}, f32[1024,1024]{1,0:T(8,128)}, u32[]{:S(2)}) copy-start(f32[1024,1024]{1,0:T(8,128)} %param.5) | copy-start | bytes 12582916
  211.4 4.8 %copy-start.10 = (f32[256,1024]{1,0:T(8,128)S(1)}, f32[256,1024]{1,0:T(8,128)}, u32[]{:S(2)}) copy-start(f32[256,1024]{1,0:T(8,128)} %all-reduce.9.cloned.1.call-done) | copy-start | bytes 3145732
  220.9 40.9 %copy-start.13 = (f32[1,256,1024]{2,1,0:T(8,128)S(1)}, f32[1,256,1024]{2,1,0:T(8,128)}, u32[]{:S(2)}) copy-start(f32[1,256,1024]{2,1,0:T(8,128)} %fusion.10) | copy-start | bytes 3145732
  220.9 40.9 %copy-start.14 = (f32[1,256,1024]{2,1,0:T(8,128)S(1)}, f32[1,256,1024]{2,1,0:T(8,128)}, u32[]{:S(2)}) copy-start(f32[1,256,1024]{2,1,0:T(8,128)} %fusion.8) | copy-start | bytes 3145732
  255.5 6.3 %copy-start.15 = (f32[1,256,1024]{2,1,0:T(8,128)S(1)}, f32[1,256,1024]{2,1,0:T(8,128)}, u32[]{:S(2)}) copy-start(f32[1,256,1024]{2,1,0:T(8,128)} %fusion.6) | copy-start | bytes 3145732
  264.1 1.9 slice-start
  264.1 2.2 copy-start.8
Sparse Core Ops, SparseCore 0:
  10.9 54.6 all-reduce.4
  78.6 51.1 all-reduce.6
  141.9 51.1 all-reduce.8
  204.3 51.1 all-reduce.10
  264.2 50.3 reduce-scatter.1
where the time goes:
time: 321 us
  waiting for transfers between devices  232 us (72%)
  matrix products  58.6 us (18%)
  between operations  14 us (4%)
  local copies, waits for them, and re-layouts  10.6 us (3%)
  other arithmetic  5.24 us (2%)
    psum x4, waiting for transfers between devices, broadcast(): return lax.psum(jnp.where(mine, array, jnp.zeros_like(array)), axis)  192 us
    reduce_scatter x1, waiting for transfers between devices, body(): lax.psum_scatter(jnp.stack(terms), 'col', scatter_dimension=1, tiled=True)  40.5 us
    dot_general x4, matrix products, body(): lax.dot_general(masked, solved, (((0,), (0,)), ((), ())), precision=hi, p...  23.3 us
    dot_general x4, matrix products, body(): lax.dot_general(solved, whitened, (((1,), (1,)), ((), ())), precision=hi,...  22.8 us
    dot_general x4, matrix products, body(): jnp.dot(diag_inverse[p].T, own, precision=hi, preferred_element_type=jnp....  12.5 us
    unnamed x32, local copies, waits for them, and re-layouts  8.3 us
  transfers between devices with their start and end apart: 5, of which 5 were waited for; matrix products, arithmetic and copies ran while one was open for 8% of the time, Pallas kernels for 0%

commit v1 on v0

--- a/solution.py
+++ b/solution.py
@@ -4,9 +4,13 @@
 from jax.sharding import PartitionSpec as P
 
 
+def process_the_vector(inputs, a_name):
+    return jnp.sum(lax.all_gather(inputs, a_name), 0)
+
+
 def broadcast(array, axis, root):
     mine = lax.axis_index(axis) == root
-    return lax.psum(jnp.where(mine, array, jnp.zeros_like(array)), axis)
+    return process_the_vector(jnp.where(mine, array, jnp.zeros_like(array)), axis)
 
 
 def grad_mask(count, natural, within, target):

time: 321 us -> 494 us (1.54); the launches traced: 321 us -> 488 us
  waiting for transfers between devices: 232 us -> 333 us
  local copies, waits for them, and re-layouts: 10.6 us -> 35.3 us
  matrix products: 58.6 us -> 81.3 us
  other arithmetic: 5.24 us -> 24.4 us
    all_gather x0 -> x4, waiting for transfers between devices: none -> 299 us  [process_the_vector(): return jnp.sum(lax.all_gather(inputs, a_name), 0)]
    psum x4 -> x0, waiting for transfers between devices: 192 us -> none  [broadcast(): return lax.psum(jnp.where(mine, array, jnp.zeros_like(array)), axis)]
    reduce_sum x0 -> x4, other arithmetic: none -> 19 us  [process_the_vector(): return jnp.sum(lax.all_gather(inputs, a_name), 0)]
    all_gather x0 -> x3, local copies, waits for them, and re-layouts: none -> 17.4 us  [process_the_vector(): return jnp.sum(lax.all_gather(inputs, a_name), 0)]
    dot_general x4, matrix products: 23.3 us -> 34.7 us  [body(): lax.dot_general(masked, solved, (((0,), (0,)), ((), ())), precision=hi, p...]
    dot_general x4, matrix products: 22.8 us -> 32 us  [body(): lax.dot_general(solved, whitened, (((1,), (1,)), ((), ())), precision=hi,...]
    reduce_sum x0 -> x3, local copies, waits for them, and re-layouts: none -> 7.85 us  [process_the_vector(): return jnp.sum(lax.all_gather(inputs, a_name), 0)]
    reduce_scatter x1, waiting for transfers between devices: 40.5 us -> 34 us  [body(): lax.psum_scatter(jnp.stack(terms), 'col', scatter_dimension=1, tiled=True)]
where the time goes in v1:
time: 494 us; the launch traced here: 488 us
  waiting for transfers between devices  333 us (67%)
  matrix products  81.3 us (16%)
  local copies, waits for them, and re-layouts  35.3 us (7%)
  other arithmetic  24.4 us (5%)
  between operations  14.4 us (3%)
    all_gather x4, waiting for transfers between devices, process_the_vector(): return jnp.sum(lax.all_gather(inputs, a_name), 0)  299 us
    dot_general x4, matrix products, body(): lax.dot_general(masked, solved, (((0,), (0,)), ((), ())), precision=hi, p...  34.7 us
    reduce_scatter x1, waiting for transfers between devices, body(): lax.psum_scatter(jnp.stack(terms), 'col', scatter_dimension=1, tiled=True)  34 us
    dot_general x4, matrix products, body(): lax.dot_general(solved, whitened, (((1,), (1,)), ((), ())), precision=hi,...  32 us
    reduce_sum x4, other arithmetic, process_the_vector(): return jnp.sum(lax.all_gather(inputs, a_name), 0)  19 us
    all_gather x3, local copies, waits for them, and re-layouts, process_the_vector(): return jnp.sum(lax.all_gather(inputs, a_name), 0)  17.4 us
    dot_general x4, matrix products, body(): jnp.dot(diag_inverse[p].T, own, precision=hi, preferred_element_type=jnp....  14.5 us
  transfers between devices with their start and end apart: 5, of which 5 were waited for; matrix products, arithmetic and copies ran while one was open for 8% of the time, Pallas kernels for 0%

profile of v1, /device:TPU:0, one launch (start us, length us, event | category | flops | bytes accessed | tf_op | source)
XLA Modules:
  0.0 488.4 jit_solution(13795338663058234936)
XLA Ops:
  7.2 0.0 all-gather.9.cloned.1.call-start
  7.2 3.3 convolution_select_fusion.3
  10.5 0.0 all-gather.9.cloned.1.call-update
  10.6 0.0 all-gather.11.cloned.1.call-start
  10.6 83.5 %all-gather.9.cloned.1.call-done = f32[1024,1024]{1,0:T(8,128)} async-done(((f32[256,1024]{1,0:T(8,128)}), f32[1024,1024]{1,0:T(8,128)}) %all-gather.9.cloned.1.call-update) | async-done | bytes 4194320 | tf_op jit(solution)/shard_map/all_gather | solution.py:8
  94.2 2.7 reduce_sum.36
  96.9 0.0 copy-start.4
  96.9 7.6 %convolution_subtract_fusion = f32[1024,1024]{1,0:T(8,128)S(1)} fusion(f32[1024,1024]{1,0:T(8,128)} %param.4, f32[256,1024]{1,0:T(8,128)S(1)} %reduce_sum.36, f32[4,256,1024]{2,1,0:T(8,128)} %param.6, pred[1024]{0:T(1024)(128)(4,1)S(1)} %fusion.56), kind=kOutput, calls=%fused_computation.5 | convolution fusion | flops 3222536192 | bytes 10486784 | tf_op jit(solution)/shard_map/dot_general | solution.py:43
  104.6 1.9 copy-done.3
  106.5 0.2 slice_select_fusion.3
  106.7 1.0 copy-done.11
  107.6 3.7 fusion.2
  111.4 0.0 all-gather.11.cloned.1.call-update
  111.4 0.0 all-gather.13.cloned.1.call-start
  111.5 79.3 %all-gather.11.cloned.1.call-done = f32[1024,1024]{0,1:T(8,128)} async-done(((f32[256,1024]{0,1:T(8,128)}), f32[1024,1024]{0,1:T(8,128)}) %all-gather.11.cloned.1.call-update) | async-done | bytes 4194320 | tf_op jit(solution)/shard_map/all_gather | solution.py:8
  190.8 5.8 %reshape.63 = f32[4,256,1024]{1,0,2:T(4,128)} reshape(f32[1024,1024]{0,1:T(8,128)} %all-gather.11.cloned.1.call-done) | data formatting | bytes 8388608 | tf_op jit(solution)/shard_map/all_gather | solution.py:8
  196.5 0.0 slice-start.2
  196.6 5.8 %reduce_sum.37 = f32[256,1024]{0,1:T(8,128)} reduce(f32[4,256,1024]{1,0,2:T(4,128)} %reshape.63, f32[]{:T(128)} %constant.74.clone.1), dimensions={0}, to_apply=%region_1.2 | reduce | flops 786432 | bytes 5242884 | tf_op jit(solution)/shard_map/reduce_sum | solution.py:8
  202.4 2.5 copy.6
  204.9 0.0 slice-done.2
  204.9 8.9 %maximum_subtract_fusion = f32[1024,1024]{1,0:T(8,128)S(1)} fusion(f32[256,1024]{1,0:T(8,128)} %copy-done.11, f32[768,1024]{1,0:T(8,128)S(1)} %slice-done.2, f32[256,1024]{0,1:T(8,128)} %reduce_sum.37, f32[4,256,1024]{2,1,0:T(8,128)} %param.6, pred[1024]{0:T(1024)(128)(4,1)S(1)} %fusion.55), kind=kOutput, calls=%fused_computation | convolution fusion | flops 3223584768 | bytes 10486784 | tf_op jit(solution)/shard_map/dot_general | solution.py:43
  213.9 0.0 copy-start.2
  213.9 1.9 copy-done.2
  215.8 0.0 copy-done.13
  215.8 0.1 slice_select_fusion.2
  216.0 0.0 copy-start.10
  216.0 1.0 copy-done.10
  216.9 3.7 fusion.1
  220.7 0.0 all-gather.13.cloned.1.call-update
  220.7 0.0 all-gather.15.cloned.1.call-start
  220.8 79.3 %all-gather.13.cloned.1.call-done = f32[1024,1024]{0,1:T(8,128)} async-done(((f32[256,1024]{0,1:T(8,128)}), f32[1024,1024]{0,1:T(8,128)}) %all-gather.13.cloned.1.call-update) | async-done | bytes 4194320 | tf_op jit(solution)/shard_map/all_gather | solution.py:8
  300.1 6.0 %reshape.64 = f32[4,256,1024]{1,0,2:T(4,128)} reshape(f32[1024,1024]{0,1:T(8,128)} %all-gather.13.cloned.1.call-done) | data formatting | bytes 8388608 | tf_op jit(solution)/shard_map/all_gather | solution.py:8
  306.1 0.0 slice-start.1
  306.1 5.8 %reduce_sum.38 = f32[256,1024]{0,1:T(8,128)} reduce(f32[4,256,1024]{1,0,2:T(4,128)} %reshape.64, f32[]{:T(128)} %constant.74.clone.1), dimensions={0}, to_apply=%region_2.3 | reduce | flops 786432 | bytes 5242884 | tf_op jit(solution)/shard_map/reduce_sum | solution.py:8
  311.9 2.5 copy.7
  314.5 8.9 %maximum_subtract_fusion.1 = f32[1024,1024]{1,0:T(8,128)S(1)} fusion(f32[256,1024]{1,0:T(8,128)} %copy-done.10, f32[768,1024]{1,0:T(8,128)S(1)} %slice-done.1, f32[256,1024]{0,1:T(8,128)} %reduce_sum.38, f32[4,256,1024]{2,1,0:T(8,128)} %param.6, pred[1024]{0:T(1024)(128)(4,1)S(1)} %fusion.54), kind=kOutput, calls=%fused_computation.1 | convolution fusion | flops 3223584768 | bytes 10486784 | tf_op jit(solution)/shard_map/dot_general | solution.py:43
  323.4 1.9 copy-done.1
  325.4 0.1 slice_select_fusion.1
  325.5 0.0 copy-start.9
  325.5 1.0 copy-done.9
  326.5 3.7 fusion
  330.2 0.0 all-gather.15.cloned.1.call-update
  330.3 0.0 reduce-scatter.2.cloned.1.call-start
  330.3 0.0 copy-start
  330.4 6.2 %fusion.10 = f32[1,256,1024]{2,1,0:T(8,128)S(1)} fusion(f32[256,1024]{1,0:T(8,128)S(1)} %copy-done.5, f32[1024,1024]{1,0:T(8,128)} %param.5, s32[1024]{0:T(1024)S(1)} %fusion.40, pred[1024]{0:T(1024)(128)(4,1)S(1)} %get-tuple-element.5, pred[1024]{0:T(1024)(128)(4,1)S(1)} %fusion.56), kind=kOutput, calls=%fused_computation.24 | convolution fusion | flops 3222536192 | bytes 6297600 | tf_op jit(solution)/shard_map/dot_general | solution.py:53
  336.6 8.0 %fusion.8 = f32[1,256,1024]{2,1,0:T(8,128)} fusion(f32[256,1024]{0,1:T(8,128)S(1)} %copy-done.6, f32[1024,1024]{1,0:T(8,128)S(1)} %copy-done, s32[1024]{0:T(1024)S(1)} %fusion.40, pred[1024]{0:T(1024)(128)(4,1)S(1)} %get-tuple-element.4, pred[1024]{0:T(1024)(128)(4,1)S(1)} %fusion.55), kind=kOutput, calls=%fused_computation.21 | convolution fusion | flops 3222536192 | bytes 6297600 | tf_op jit(solution)/shard_map/dot_general | solution.py:53
  344.7 8.3 %fusion.6 = f32[1,256,1024]{2,1,0:T(8,128)} fusion(f32[256,1024]{0,1:T(8,128)S(1)} %copy-done.7, f32[1024,1024]{1,0:T(8,128)S(1)} %copy-done, s32[1024]{0:T(1024)S(1)} %fusion.40, pred[1024]{0:T(1024)(128)(4,1)S(1)} %get-tuple-element.3, pred[1024]{0:T(1024)(128)(4,1)S(1)} %fusion.54), kind=kOutput, calls=%fused_computation.18 | convolution fusion | flops 3222536192 | bytes 6297600 | tf_op jit(solution)/shard_map/dot_general | solution.py:53
  353.0 56.7 %all-gather.15.cloned.1.call-done = f32[1024,1024]{0,1:T(8,128)} async-done(((f32[256,1024]{0,1:T(8,128)}), f32[1024,1024]{0,1:T(8,128)}) %all-gather.15.cloned.1.call-update) | async-done | bytes 4194320 | tf_op jit(solution)/shard_map/all_gather | solution.py:8
  409.6 5.6 %reshape.65 = f32[4,256,1024]{1,0,2:T(4,128)} reshape(f32[1024,1024]{0,1:T(8,128)} %all-gather.15.cloned.1.call-done) | data formatting | bytes 8388608 | tf_op jit(solution)/shard_map/all_gather | solution.py:8
  415.3 4.7 reduce_sum.39
  419.9 0.0 copy-start.8
  420.0 9.5 %fusion.4 = f32[1,256,1024]{2,1,0:T(8,128)S(1)} fusion(f32[256,1024]{0,1:T(8,128)S(1)} %reduce_sum.39, f32[1024,1024]{1,0:T(8,128)} %param.5, s32[1024]{0:T(1024)S(1)} %fusion.40, pred[1024]{0:T(1024)(128)(4,1)S(1)} %get-tuple-element.2, pred[1024]{0:T(1024)(128)(4,1)S(1)} %fusion.53), kind=kOutput, calls=%fused_computation.15 | convolution fusion | flops 3222536192 | bytes 6297600 | tf_op jit(solution)/shard_map/dot_general | solution.py:53
  429.5 2.3 pad_maximum_fusion.1
  431.8 0.0 reduce-scatter.2.cloned.1.call-update
  431.8 0.0 slice-start
  431.8 2.8 copy.8
  434.6 0.0 slice-done
  434.6 9.2 %maximum_subtract_fusion.2 = f32[1024,1024]{1,0:T(8,128)S(1)} fusion(f32[256,1024]{1,0:T(8,128)} %copy-done.9, f32[768,1024]{1,0:T(8,128)S(1)} %slice-done, f32[256,1024]{0,1:T(8,128)} %copy-done.8, f32[4,256,1024]{2,1,0:T(8,128)} %param.6, pred[1024]{0:T(1024)(128)(4,1)S(1)} %fusion.53), kind=kOutput, calls=%fused_computation.2 | convolution fusion | flops 3223584768 | bytes 10486784 | tf_op jit(solution)/shard_map/dot_general | solution.py:43
  443.8 0.0 copy-start.12
  443.8 0.4 slice.74
  444.2 0.9 copy-done.12
  445.1 0.2 slice_select_fusion
  445.3 2.3 pad_maximum_fusion
  447.6 34.0 %reduce-scatter.2.cloned.1.call-done = f32[4,32,1024]{2,1,0:T(8,128)} async-done(((f32[4,256,1024]{2,1,0:T(8,128)}), f32[4,32,1024]{2,1,0:T(8,128)}) %reduce-scatter.2.cloned.1.call-update) | async-done | bytes 524304 | tf_op jit(solution)/shard_map/reduce_scatter | solution.py:61
  (27 shorter events, 0.1 us)
Async XLA Ops:
  7.2 87.0 %all-gather.9.cloned.1.call-start = ((), (), s32[]{:S(2)}) async-start(), calls=%async_computation.2 | async-start | bytes 5242880 | tf_op jit(solution)/shard_map/all_gather | solution.py:8
  10.6 180.2 %all-gather.11.cloned.1.call-start = ((), (), s32[]{:S(2)}) async-start(), calls=%async_computation.3 | async-start | bytes 5242880 | tf_op jit(solution)/shard_map/all_gather | solution.py:8
  96.9 7.6 %copy-start.4 = (f32[256,1024]{1,0:T(8,128)}, f32[256,1024]{1,0:T(8,128)S(1)}, u32[]{:S(2)}) copy-start(f32[256,1024]{1,0:T(8,128)S(1)} %reduce_sum.36) | copy-start | bytes 3145732
  104.6 1.9 copy-start.3
  106.6 1.0 copy-start.11
  111.4 188.7 %all-gather.13.cloned.1.call-start = ((), (), s32[]{:S(2)}) async-start(), calls=%async_computation.4 | async-start | bytes 5242880 | tf_op jit(solution)/shard_map/all_gather | solution.py:8
  196.5 8.4 %slice-start.2 = ((f32[1024,1024]{1,0:T(8,128)}), f32[768,1024]{1,0:T(8,128)S(1)}, s32[]{:S(2)}) async-start(f32[1024,1024]{1,0:T(8,128)} %copy-done.3), calls=%async_computation.8 | async-start | bytes 6291456 | tf_op jit(solution)/shard_map/slice | solution.py:52
  204.9 10.9 %copy-start.13 = (f32[256,1024]{1,0:T(8,128)S(1)}, f32[256,1024]{1,0:T(8,128)}, u32[]{:S(2)}) copy-start(f32[256,1024]{1,0:T(8,128)} %copy.6) | copy-start | bytes 3145732
  213.9 1.9 copy-start.2
  216.0 1.0 copy-start.10
  220.7 188.9 %all-gather.15.cloned.1.call-start = ((), (), s32[]{:S(2)}) async-start(), calls=%async_computation.5 | async-start | bytes 5242880 | tf_op jit(solution)/shard_map/all_gather | solution.py:8
  306.1 8.4 %slice-start.1 = ((f32[1024,1024]{1,0:T(8,128)}), f32[768,1024]{1,0:T(8,128)S(1)}, s32[]{:S(2)}) async-start(f32[1024,1024]{1,0:T(8,128)} %copy-done.2), calls=%async_computation.7 | async-start | bytes 6291456 | tf_op jit(solution)/shard_map/slice | solution.py:52
  314.5 10.9 %copy-start.14 = (f32[256,1024]{1,0:T(8,128)S(1)}, f32[256,1024]{1,0:T(8,128)}, u32[]{:S(2)}) copy-start(f32[256,1024]{1,0:T(8,128)} %copy.7) | copy-start | bytes 3145732
  323.4 1.9 copy-start.1
  325.4 5.0 %copy-start.5 = (f32[256,1024]{1,0:T(8,128)S(1)}, f32[256,1024]{1,0:T(8,128)}, u32[]{:S(2)}) copy-start(f32[256,1024]{1,0:T(8,128)} %copy-done.4) | copy-start | bytes 3145732
  325.5 1.0 copy-start.9
  330.2 6.4 %copy-start.6 = (f32[256,1024]{0,1:T(8,128)S(1)}, f32[256,1024]{0,1:T(8,128)}, u32[]{:S(2)}) copy-start(f32[256,1024]{0,1:T(8,128)} %reduce_sum.37) | copy-start | bytes 3145732
  330.3 151.4 %reduce-scatter.2.cloned.1.call-start = ((), (), s32[]{:S(2)}) async-start(), calls=%async_computation.1 | async-start | bytes 4718592 | tf_op jit(solution)/shard_map/reduce_scatter | solution.py:61
  330.3 6.3 %copy-start = (f32[1024,1024]{1,0:T(8,128)S(1)}, f32[1024,1024]{1,0:T(8,128)}, u32[]{:S(2)}) copy-start(f32[1024,1024]{1,0:T(8,128)} %param.5) | copy-start | bytes 12582916
  336.6 8.1 %copy-start.7 = (f32[256,1024]{0,1:T(8,128)S(1)}, f32[256,1024]{0,1:T(8,128)}, u32[]{:S(2)}) copy-start(f32[256,1024]{0,1:T(8,128)} %reduce_sum.38) | copy-start | bytes 3145732
  419.9 11.8 %copy-start.8 = (f32[256,1024]{0,1:T(8,128)}, f32[256,1024]{0,1:T(8,128)S(1)}, u32[]{:S(2)}) copy-start(f32[256,1024]{0,1:T(8,128)S(1)} %reduce_sum.39) | copy-start | bytes 3145732
  420.0 9.5 %copy-start.15 = (f32[1,256,1024]{2,1,0:T(8,128)S(1)}, f32[1,256,1024]{2,1,0:T(8,128)}, u32[]{:S(2)}) copy-start(f32[1,256,1024]{2,1,0:T(8,128)} %fusion.8) | copy-start | bytes 3145732
  420.0 9.5 %copy-start.16 = (f32[1,256,1024]{2,1,0:T(8,128)S(1)}, f32[1,256,1024]{2,1,0:T(8,128)}, u32[]{:S(2)}) copy-start(f32[1,256,1024]{2,1,0:T(8,128)} %fusion.6) | copy-start | bytes 3145732
  431.8 2.8 slice-start
  443.8 1.3 copy-start.12
Sparse Core Ops, SparseCore 0:
  10.7 83.4 all-gather.8
  111.5 79.2 all-gather.10
  220.8 79.2 all-gather.12
  330.4 79.2 all-gather.14
  431.9 49.6 reduce-scatter.1
